TPU v7x, 512 devices: a whole 4x8x8 slice. The times are simulated.
512 devices in a mesh: tm: 32 (over y, x), chan: 16 (over z, core).
Axes of the slice: x: 4, y: 8, z: 8, core: 2. Of those that a mesh axis runs over, the one named last changes fastest.
Arguments:
- record: bfloat16 [32768, 10240], P('tm', 'chan'), may hold values from -6 to 6
- fir_taps: bfloat16 [64], replicated, may hold values from -0.75 to 0.75
- gauge_lag: int32 [10240], P('chan'), may hold values from 1 to 16
- projector: bfloat16 [32768, 128], P('tm'), may hold values from -0.1875 to 0.1875
- compress: float32 [256, 128], replicated, may hold values from -0.5 to 0.5
Outputs:
- sketch: float32 [128, 10240], P('tm', 'chan')
Inputs may be any that keep to these rules, and one draw needn't show every extreme that they name: `gauge_lag`: some channel has lag 16.
All inputs are finite; a program needn't handle non-finite values.
Results may differ from a plain program's by a relative error of at most 0.0028.
Values may be sent and summed in bfloat16 or wider, within the bound.
A program may use at most 64 MiB of HBM per device.

v0:
```python
import jax
import jax.numpy as jnp
from jax import lax
from jax.sharding import PartitionSpec as P

TAPS = 64
GAUGE_MAX = 16
K_ITERS = 8


def from_behind(value, axis, steps):
    count = lax.axis_size(axis)
    first, last = (max(0, -steps), min(count, count - steps))
    return lax.ppermute(value, axis, [(source, source + steps) for source in range(first, last)])


def from_partner(value, axis, bit):
    mask = 2**bit
    pairs = [(source, source ^ mask) for source in range(lax.axis_size(axis))]
    return lax.ppermute(value, axis, pairs)


def toeplitz_block(fir_taps, out_count):
    row_ids = jnp.arange(out_count, dtype=jnp.int32)[:, None]
    col_ids = jnp.arange(out_count + TAPS - 1, dtype=jnp.int32)[None, :]
    offset = row_ids + TAPS - 1 - col_ids
    tap_ids = jnp.arange(TAPS, dtype=jnp.int32)
    onehot = (offset[:, :, None] == tap_ids[None, None, :]).astype(jnp.float32)
    return jnp.sum(onehot * fir_taps.astype(jnp.float32)[None, None, :], axis=2).astype(
        jnp.bfloat16
    )


def filter_mix(gram, compress):
    width = gram.shape[0]
    eye = jnp.eye(width, dtype=jnp.float32)
    mean_level = jnp.trace(gram) / width
    shifted = gram - mean_level * eye
    signed = shifted / jnp.sqrt(jnp.sum(shifted * shifted) + 1e-06)
    for step_index in range(K_ITERS):
        square = jnp.dot(
            signed, signed, precision=lax.Precision.HIGHEST, preferred_element_type=jnp.float32
        )
        signed = jnp.dot(
            signed,
            1.5 * eye - 0.5 * square,
            precision=lax.Precision.HIGHEST,
            preferred_element_type=jnp.float32,
        )
    filter_mat = 0.5 * (eye + signed)
    return jnp.dot(
        compress.T, filter_mat, precision=lax.Precision.HIGHEST, preferred_element_type=jnp.float32
    )


def inner_rows(first_mat, second_mat):
    return jnp.dot(
        first_mat, second_mat.T, precision=lax.Precision.HIGHEST, preferred_element_type=jnp.float32
    )


def on_device(record, fir_taps, gauge_lag, projector, compress):
    sample_rows = record.shape[0]
    column_count = record.shape[1]
    halo_rows = TAPS - 1 + GAUGE_MAX
    tail_rows = record[sample_rows - halo_rows :]
    before = from_behind(tail_rows, "tm", 1)
    extended = jnp.concatenate([before, record], 0)
    lead_matrix = toeplitz_block(fir_taps, GAUGE_MAX)
    lead_part = jnp.dot(
        lead_matrix, extended[: GAUGE_MAX + TAPS - 1], preferred_element_type=jnp.float32
    )
    block_rows = min(128, sample_rows)
    main_matrix = toeplitz_block(fir_taps, block_rows)

    def filter_block(block_index):
        segment = lax.dynamic_slice_in_dim(
            extended, GAUGE_MAX + block_index * block_rows, block_rows + TAPS - 1, 0
        )
        return jnp.dot(main_matrix, segment, preferred_element_type=jnp.float32)

    main_part = lax.map(filter_block, jnp.arange(sample_rows // block_rows, dtype=jnp.int32))
    filtered = jnp.concatenate([lead_part, main_part.reshape(sample_rows, column_count)], 0)
    current = filtered[GAUGE_MAX:]
    lagged = jnp.zeros((sample_rows, column_count), jnp.float32)
    for lag_step in range(1, GAUGE_MAX + 1):
        chosen = (gauge_lag == lag_step).astype(jnp.float32)[None, :]
        lagged = (
            lagged + chosen * filtered[GAUGE_MAX - lag_step : GAUGE_MAX - lag_step + sample_rows]
        )
    strain = (current - lagged).astype(jnp.bfloat16)
    sketch = lax.dot_general(
        projector, strain, (((0,), (0,)), ((), ())), preferred_element_type=jnp.float32
    )
    depth_count = lax.axis_size("tm").bit_length() - 1
    position = lax.axis_index("tm")
    for depth_level in range(depth_count):
        is_lower = position // 2**depth_level % 2 == 0
        partner = from_partner(sketch, "tm", depth_level)
        stacked = jnp.where(
            is_lower, jnp.concatenate([sketch, partner], 0), jnp.concatenate([partner, sketch], 0)
        )
        gram = lax.psum(inner_rows(stacked, stacked), "chan")
        mixing = filter_mix(gram, compress)
        sketch = jnp.dot(
            mixing, stacked, precision=lax.Precision.HIGHEST, preferred_element_type=jnp.float32
        )
    share_rows = sketch.shape[0] // lax.axis_size("tm")
    return lax.dynamic_slice_in_dim(sketch, position * share_rows, share_rows, 0)


def solution(mesh):
    return jax.shard_map(
        on_device,
        mesh=mesh,
        in_specs=(P("tm", "chan"), P(), P("chan"), P("tm", None), P()),
        out_specs=P("tm", "chan"),
        check_vma=False,
    )
```

profile of v0, /device:TPU:1, one launch (start us, length us, event | category | flops | bytes accessed | tf_op | source)
XLA Modules:
  0.0 803.2 jit_solution(263706194352711852)
XLA Ops:
  6.5 1.0 slice.51
  7.5 3.9 collective-permute-start
  12.2 2.0 select_reduce_fusion
  15.2 1.6 pad_maximum_fusion.1
  16.9 19.6 %while.12 = (s32[]{:T(128)}, f32[8,128,640]{2,1,0:T(8,128)}, s32[8]{0:T(128)S(1)}, bf16[1103,640]{1,0:T(8,128)(2,1)S(1)}, bf16[128,191]{1,0:T(8,128)(2,1)S(1)}, ...) while((s32[]{:T(128)}, f32[8,128,640]{2,1,0:T(8,128)}, s32[8]{0:T(128)S(1)}, ...), condition=%wide.region_2.3_spmd, body=%wide.region_1.0_spmd.sunk | while | flops 31293448 | bytes 1949883 | solution.py:82
  25.9 0.8 constant_dynamic-update-slice_fusion.2
  28.4 0.8 constant_dynamic-update-slice_fusion.2
  36.6 24.8 %fusion.52 = f32[128,640]{1,0:T(8,128)S(1)} fusion(bf16[1024,128]{1,0:T(8,128)(2,1)S(1)} %copy-done, f32[1024,640]{1,0:T(8,128)} %bitcast.181, f32[16,640]{1,0:T(8,128)S(1)} %fusion.158, f32[640]{0:T(1024)S(1)} %get-tuple-element.100, f32[640]{0:T(1024)S(1)} %get-tuple-element.101, f32[640]{0:T(1024)S(1)} %get-tuple-element.87, ...), kind=kOutput, calls=%fused_computation.121 | convolution fusion | flops 199884800 | bytes 3293184 | tf_op jit(solution)/shard_map/dot_general | solution.py:92
  61.4 3.1 collective-permute-start.1
  64.6 4.7 collective-permute-done.1
  69.3 1.5 fusion.69
  71.4 123.7 %all-reduce.6.cloned.1.call-done = f32[256,256]{1,0:T(8,128)} async-done(((f32[256,256]{1,0:T(8,128)}), f32[256,256]{1,0:T(8,128)}) %all-reduce.6.cloned.1.call-update) | async-done | bytes 262160 | tf_op jit(solution)/shard_map/psum | solution.py:103
  195.1 1.6 select_reduce_fusion.6
  197.4 1.6 multiply_reduce_fusion.4
  199.7 1.5 select_subtract_fusion.39
  201.1 1.4 fusion.97
  209.1 4.6 collective-permute-start.2
  213.8 7.4 collective-permute-done.2
  221.2 1.5 fusion.67
  223.0 115.3 %all-reduce.8.cloned.1.call-done = f32[256,256]{1,0:T(8,128)} async-done(((f32[256,256]{1,0:T(8,128)}), f32[256,256]{1,0:T(8,128)}) %all-reduce.8.cloned.1.call-update) | async-done | bytes 262160 | tf_op jit(solution)/shard_map/psum | solution.py:103
  338.3 1.6 select_reduce_fusion.5
  340.5 1.6 multiply_reduce_fusion.3
  342.8 1.5 select_subtract_fusion.31
  344.3 1.3 fusion.94
  352.3 3.1 collective-permute-start.3
  355.4 7.4 collective-permute-done.3
  362.8 1.5 fusion.65
  364.6 115.3 %all-reduce.10.cloned.1.call-done = f32[256,256]{1,0:T(8,128)} async-done(((f32[256,256]{1,0:T(8,128)}), f32[256,256]{1,0:T(8,128)}) %all-reduce.10.cloned.1.call-update) | async-done | bytes 262160 | tf_op jit(solution)/shard_map/psum | solution.py:103
  479.9 1.6 select_reduce_fusion.4
  482.2 1.6 multiply_reduce_fusion.2
  484.5 1.5 select_subtract_fusion.23
  486.0 1.4 fusion.91
  493.9 4.0 collective-permute-start.4
  498.0 14.5 %collective-permute-done.4 = f32[128,640]{1,0:T(8,128)S(1)} collective-permute-done((f32[128,640]{1,0:T(8,128)S(1)}, f32[128,640]{1,0:T(8,128)S(1)}, u32[]{:S(2)}, u32[]{:S(2)}) %collective-permute-start.4) | collective-permute-done | bytes 327712 | tf_op jit(solution)/shard_map/ppermute | solution.py:20
  512.5 1.5 fusion.63
  514.3 115.4 %all-reduce.12.cloned.1.call-done = f32[256,256]{1,0:T(8,128)} async-done(((f32[256,256]{1,0:T(8,128)}), f32[256,256]{1,0:T(8,128)}) %all-reduce.12.cloned.1.call-update) | async-done | bytes 262160 | tf_op jit(solution)/shard_map/psum | solution.py:103
  629.7 1.6 select_reduce_fusion.3
  631.9 1.6 multiply_reduce_fusion.1
  634.3 1.4 select_subtract_fusion.15
  635.7 1.3 fusion.88
  643.7 7.4 collective-permute-start.5
  651.1 8.9 %collective-permute-done.5 = f32[128,640]{1,0:T(8,128)S(1)} collective-permute-done((f32[128,640]{1,0:T(8,128)S(1)}, f32[128,640]{1,0:T(8,128)S(1)}, u32[]{:S(2)}, u32[]{:S(2)}) %collective-permute-start.5) | collective-permute-done | bytes 327712 | tf_op jit(solution)/shard_map/ppermute | solution.py:20
  660.0 1.5 fusion.61
  661.6 120.0 %all-reduce.14.cloned.1.call-done = f32[256,256]{1,0:T(8,128)} async-done(((f32[256,256]{1,0:T(8,128)}), f32[256,256]{1,0:T(8,128)}) %all-reduce.14.cloned.1.call-update) | async-done | bytes 262160 | tf_op jit(solution)/shard_map/psum | solution.py:103
  781.6 1.6 select_reduce_fusion.2
  783.8 1.6 multiply_reduce_fusion
  786.1 1.5 select_subtract_fusion.7
  787.6 1.3 fusion.85
  (137 shorter events, 49.3 us)
Async XLA Ops:
  6.5 30.1 %copy-start = (bf16[1024,128]{1,0:T(8,128)(2,1)S(1)}, bf16[1024,128]{1,0:T(8,128)(2,1)}, u32[]{:S(2)}) copy-start(bf16[1024,128]{1,0:T(8,128)(2,1)} %param.10) | copy-start | bytes 786436
  6.5 188.6 %all-reduce.6.cloned.1.call-start = ((), (), s32[]{:S(2)}) async-start(), calls=%async_computation | async-start | bytes 524288 | tf_op jit(solution)/shard_map/psum | solution.py:103
  7.5 7.7 collective-permute-start
  61.4 7.8 collective-permute-start.1
  70.8 267.5 %all-reduce.8.cloned.1.call-start = ((), (), s32[]{:S(2)}) async-start(), calls=%async_computation.1 | async-start | bytes 524288 | tf_op jit(solution)/shard_map/psum | solution.py:103
  205.2 2.7 copy-start.1
  209.1 12.1 %collective-permute-start.2 = (f32[128,640]{1,0:T(8,128)S(1)}, f32[128,640]{1,0:T(8,128)S(1)}, u32[]{:S(2)}, u32[]{:S(2)}) collective-permute-start(f32[128,640]{1,0:T(8,128)S(1)} %fusion.68), channel_id=1, source_target_pairs={{0,32},{16,48},{32,0},{48,16},{64,96},{80,112},{96,64},{112,80},{1... | collective-permute-start | bytes 983048 | tf_op jit(solution)/shard_map/ppermute | solution.py:20
  222.7 257.2 %all-reduce.10.cloned.1.call-start = ((), (), s32[]{:S(2)}) async-start(), calls=%async_computation.2 | async-start | bytes 524288 | tf_op jit(solution)/shard_map/psum | solution.py:103
  352.3 10.5 %collective-permute-start.3 = (f32[128,640]{1,0:T(8,128)S(1)}, f32[128,640]{1,0:T(8,128)S(1)}, u32[]{:S(2)}, u32[]{:S(2)}) collective-permute-start(f32[128,640]{1,0:T(8,128)S(1)} %fusion.66), channel_id=1, source_target_pairs={{0,64},{16,80},{32,96},{48,112},{64,0},{80,16},{96,32},{112,48},{1... | collective-permute-start | bytes 983048 | tf_op jit(solution)/shard_map/ppermute | solution.py:20
  364.4 265.3 %all-reduce.12.cloned.1.call-start = ((), (), s32[]{:S(2)}) async-start(), calls=%async_computation.3 | async-start | bytes 524288 | tf_op jit(solution)/shard_map/psum | solution.py:103
  493.9 18.5 %collective-permute-start.4 = (f32[128,640]{1,0:T(8,128)S(1)}, f32[128,640]{1,0:T(8,128)S(1)}, u32[]{:S(2)}, u32[]{:S(2)}) collective-permute-start(f32[128,640]{1,0:T(8,128)S(1)} %fusion.64), channel_id=1, source_target_pairs={{0,128},{16,144},{32,160},{48,176},{64,192},{80,208},{96,224},{112... | collective-permute-start | bytes 983048 | tf_op jit(solution)/shard_map/ppermute | solution.py:20
  514.0 267.6 %all-reduce.14.cloned.1.call-start = ((), (), s32[]{:S(2)}) async-start(), calls=%async_computation.4 | async-start | bytes 524288 | tf_op jit(solution)/shard_map/psum | solution.py:103
  643.7 16.3 %collective-permute-start.5 = (f32[128,640]{1,0:T(8,128)S(1)}, f32[128,640]{1,0:T(8,128)S(1)}, u32[]{:S(2)}, u32[]{:S(2)}) collective-permute-start(f32[128,640]{1,0:T(8,128)S(1)} %fusion.62), channel_id=1, source_target_pairs={{0,256},{16,272},{32,288},{48,304},{64,320},{80,336},{96,352},{112... | collective-permute-start | bytes 983048 | tf_op jit(solution)/shard_map/ppermute | solution.py:20
Sparse Core Ops, SparseCore 0:
  70.9 124.1 all-reduce.5
  222.9 115.3 all-reduce.7
  364.5 115.3 all-reduce.9
  514.1 115.5 all-reduce.11
  661.7 119.8 all-reduce.13
where the time goes:
time: 809 us; the launch traced here: 803 us
  waiting for transfers between devices  633 us (78%)
  matrix products  81.5 us (10%)
  starting transfers between devices  27.5 us (3%)
  other arithmetic  21.4 us (3%)
  between operations  21.3 us (3%)
  local copies, waits for them, and re-layouts  13.8 us (2%)
    psum x5, waiting for transfers between devices, on_device(): gram = lax.psum(inner_rows(stacked, stacked), 'chan')  590 us
    ppermute x5, waiting for transfers between devices, from_partner(): return lax.ppermute(value, axis, pairs)  42.9 us
    dot_general x1, matrix products, on_device(): lax.dot_general(projector, strain, (((0,), (0,)), ((), ())), preferred_el...  24.8 us
    ppermute x5, starting transfers between devices, from_partner(): return lax.ppermute(value, axis, pairs)  22.3 us
    dot_general x40, matrix products, filter_mix(): jnp.dot(signed, signed, precision=lax.Precision.HIGHEST, preferred_elemen...  20.5 us
    dot_general x40, matrix products, filter_mix(): jnp.dot(signed, 1.5 * eye - 0.5 * square, precision=lax.Precision.HIGHEST...  20 us
  transfers between devices with their start and end apart: 11, of which 10 were waited for; matrix products, arithmetic and copies ran while one was open for 0% of the time, Pallas kernels for 0%

commit v1 on v0

--- a/solution.py
+++ b/solution.py
@@ -100,7 +100,7 @@
         stacked = jnp.where(
             is_lower, jnp.concatenate([sketch, partner], 0), jnp.concatenate([partner, sketch], 0)
         )
-        gram = lax.psum(inner_rows(stacked, stacked), "chan")
+        gram = jnp.sum(lax.all_gather(inner_rows(stacked, stacked), "chan"), axis=0)
         mixing = filter_mix(gram, compress)
         sketch = jnp.dot(
             mixing, stacked, precision=lax.Precision.HIGHEST, preferred_element_type=jnp.float32

time: 809 us -> 446 us (0.55)
  waiting for transfers between devices: 633 us -> 278 us
  matrix products: 81.5 us -> 71.4 us
    psum x5 -> x0, waiting for transfers between devices: 590 us -> none  [on_device(): gram = lax.psum(inner_rows(stacked, stacked), 'chan')]
    all_gather x0 -> x5, waiting for transfers between devices: none -> 231 us  [on_device(): gram = jnp.sum(lax.all_gather(inner_rows(stacked, stacked), 'chan'), axis=0)]
    reduce_sum x0 -> x5, other arithmetic: none -> 12.4 us  [on_device(): gram = jnp.sum(lax.all_gather(inner_rows(stacked, stacked), 'chan'), axis=0)]
  transfers between devices with their start and end apart: 11 -> 11, of which waited for: 10 -> 10; matrix products, arithmetic and copies ran while one was open for 0% -> 1% of each run, Pallas kernels for 0% -> 0%
where the time goes in v1:
time: 446 us; the launch traced here: 441 us
  waiting for transfers between devices  278 us (62%)
  matrix products  71.4 us (16%)
  starting transfers between devices  27 us (6%)
  other arithmetic  24.2 us (5%)
  between operations  21.3 us (5%)
  local copies, waits for them, and re-layouts  13.8 us (3%)
  loops' own time  5.11 us (1%)
    all_gather x5, waiting for transfers between devices, on_device(): gram = jnp.sum(lax.all_gather(inner_rows(stacked, stacked), 'chan'), axis=0)  231 us
    ppermute x5, waiting for transfers between devices, from_partner(): return lax.ppermute(value, axis, pairs)  46.7 us
    dot_general x1, matrix products, on_device(): lax.dot_general(projector, strain, (((0,), (0,)), ((), ())), preferred_el...  24.8 us
    ppermute x5, starting transfers between devices, from_partner(): return lax.ppermute(value, axis, pairs)  21.7 us
    dot_general x40, matrix products, filter_mix(): jnp.dot(signed, signed, precision=lax.Precision.HIGHEST, preferred_elemen...  15.3 us
    dot_general x40, matrix products, filter_mix(): jnp.dot(signed, 1.5 * eye - 0.5 * square, precision=lax.Precision.HIGHEST...  15.2 us
    reduce_sum x5, other arithmetic, on_device(): gram = jnp.sum(lax.all_gather(inner_rows(stacked, stacked), 'chan'), axis=0)  12.4 us
  transfers between devices with their start and end apart: 11, of which 10 were waited for; matrix products, arithmetic and copies ran while one was open for 1% of the time, Pallas kernels for 0%

profile of v1, /device:TPU:1, one launch (start us, length us, event | category | flops | bytes accessed | tf_op | source)
XLA Modules:
  0.0 440.9 jit_solution(13508083316437326486)
XLA Ops:
  6.5 1.0 slice.51
  7.5 3.9 collective-permute-start
  11.5 0.7 convert_element_type.79
  12.2 2.0 select_reduce_fusion
  14.4 0.7 compare_convert_fusion.15
  15.3 1.6 pad_maximum_fusion.1
  16.9 19.6 %while.12 = (s32[]{:T(128)}, f32[8,128,640]{2,1,0:T(8,128)}, s32[8]{0:T(128)S(1)}, bf16[1103,640]{1,0:T(8,128)(2,1)S(1)}, bf16[128,191]{1,0:T(8,128)(2,1)S(1)}, ...) while((s32[]{:T(128)}, f32[8,128,640]{2,1,0:T(8,128)}, s32[8]{0:T(128)S(1)}, ...), condition=%wide.region_2.3_spmd, body=%wide.region_1.0_spmd.sunk | while | flops 31293448 | bytes 1949883 | solution.py:82
  18.6 0.7 constant_dynamic-update-slice_fusion.2
  21.1 0.8 constant_dynamic-update-slice_fusion.2
  23.5 0.8 constant_dynamic-update-slice_fusion.2
  26.0 0.8 constant_dynamic-update-slice_fusion.2
  28.4 0.8 constant_dynamic-update-slice_fusion.2
  30.9 0.7 constant_dynamic-update-slice_fusion.2
  33.3 0.8 constant_dynamic-update-slice_fusion.2
  35.8 0.7 constant_dynamic-update-slice_fusion.2
  36.7 24.8 %fusion.52 = f32[128,640]{1,0:T(8,128)S(1)} fusion(bf16[1024,128]{1,0:T(8,128)(2,1)S(1)} %copy-done, f32[1024,640]{1,0:T(8,128)} %bitcast.191, f32[16,640]{1,0:T(8,128)S(1)} %fusion.158, f32[640]{0:T(1024)S(1)} %get-tuple-element.100, f32[640]{0:T(1024)S(1)} %get-tuple-element.101, f32[640]{0:T(1024)S(1)} %get-tuple-element.87, ...), kind=kOutput, calls=%fused_computation.121 | convolution fusion | flops 199884800 | bytes 3293184 | tf_op jit(solution)/shard_map/dot_general | solution.py:92
  61.4 3.1 collective-permute-start.1
  64.6 4.7 %collective-permute-done.1 = f32[128,640]{1,0:T(8,128)S(1)} collective-permute-done((f32[128,640]{1,0:T(8,128)S(1)}, f32[128,640]{1,0:T(8,128)S(1)}, u32[]{:S(2)}, u32[]{:S(2)}) %collective-permute-start.1) | collective-permute-done | bytes 327712 | tf_op jit(solution)/shard_map/ppermute | solution.py:20
  69.3 1.5 fusion.69
  71.4 53.0 %all-gather.11.cloned.1.call-done = f32[4096,256]{1,0:T(8,128)} async-done(((f32[256,256]{1,0:T(8,128)}), f32[4096,256]{1,0:T(8,128)}) %all-gather.11.cloned.1.call-update) | async-done | bytes 4194320 | tf_op jit(solution)/shard_map/all_gather | solution.py:103
  124.4 2.5 reduce_sum.144
  128.2 0.7 multiply_reduce_fusion.4
  137.0 4.4 %collective-permute-start.2 = (f32[128,640]{1,0:T(8,128)S(1)}, f32[128,640]{1,0:T(8,128)S(1)}, u32[]{:S(2)}, u32[]{:S(2)}) collective-permute-start(f32[128,640]{1,0:T(8,128)S(1)} %fusion.68), channel_id=1, source_target_pairs={{0,32},{16,48},{32,0},{48,16},{64,96},{80,112},{96,64},{112,80},{1... | collective-permute-start | bytes 983048 | tf_op jit(solution)/shard_map/ppermute | solution.py:20
  141.4 7.9 %collective-permute-done.2 = f32[128,640]{1,0:T(8,128)S(1)} collective-permute-done((f32[128,640]{1,0:T(8,128)S(1)}, f32[128,640]{1,0:T(8,128)S(1)}, u32[]{:S(2)}, u32[]{:S(2)}) %collective-permute-start.2) | collective-permute-done | bytes 327712 | tf_op jit(solution)/shard_map/ppermute | solution.py:20
  149.4 1.5 fusion.67
  151.1 44.0 %all-gather.13.cloned.1.call-done = f32[4096,256]{1,0:T(8,128)} async-done(((f32[256,256]{1,0:T(8,128)}), f32[4096,256]{1,0:T(8,128)}) %all-gather.13.cloned.1.call-update) | async-done | bytes 4194320 | tf_op jit(solution)/shard_map/all_gather | solution.py:103
  195.1 2.5 reduce_sum.147
  197.6 0.6 select_reduce_fusion.5
  198.9 0.7 multiply_reduce_fusion.3
  207.7 2.9 collective-permute-start.3
  210.7 7.9 %collective-permute-done.3 = f32[128,640]{1,0:T(8,128)S(1)} collective-permute-done((f32[128,640]{1,0:T(8,128)S(1)}, f32[128,640]{1,0:T(8,128)S(1)}, u32[]{:S(2)}, u32[]{:S(2)}) %collective-permute-start.3) | collective-permute-done | bytes 327712 | tf_op jit(solution)/shard_map/ppermute | solution.py:20
  218.6 1.5 fusion.65
  220.4 44.0 %all-gather.15.cloned.1.call-done = f32[4096,256]{1,0:T(8,128)} async-done(((f32[256,256]{1,0:T(8,128)}), f32[4096,256]{1,0:T(8,128)}) %all-gather.15.cloned.1.call-update) | async-done | bytes 4194320 | tf_op jit(solution)/shard_map/all_gather | solution.py:103
  264.3 2.5 reduce_sum.150
  266.8 0.6 select_reduce_fusion.4
  268.1 0.7 multiply_reduce_fusion.2
  276.9 4.0 collective-permute-start.4
  281.0 14.7 %collective-permute-done.4 = f32[128,640]{1,0:T(8,128)S(1)} collective-permute-done((f32[128,640]{1,0:T(8,128)S(1)}, f32[128,640]{1,0:T(8,128)S(1)}, u32[]{:S(2)}, u32[]{:S(2)}) %collective-permute-start.4) | collective-permute-done | bytes 327712 | tf_op jit(solution)/shard_map/ppermute | solution.py:20
  295.7 1.5 fusion.63
  297.6 43.9 %all-gather.17.cloned.1.call-done = f32[4096,256]{1,0:T(8,128)} async-done(((f32[256,256]{1,0:T(8,128)}), f32[4096,256]{1,0:T(8,128)}) %all-gather.17.cloned.1.call-update) | async-done | bytes 4194320 | tf_op jit(solution)/shard_map/all_gather | solution.py:103
  341.5 2.5 reduce_sum.153
  345.2 0.7 multiply_reduce_fusion.1
  354.0 7.2 %collective-permute-start.5 = (f32[128,640]{1,0:T(8,128)S(1)}, f32[128,640]{1,0:T(8,128)S(1)}, u32[]{:S(2)}, u32[]{:S(2)}) collective-permute-start(f32[128,640]{1,0:T(8,128)S(1)} %fusion.62), channel_id=1, source_target_pairs={{0,256},{16,272},{32,288},{48,304},{64,320},{80,336},{96,352},{112... | collective-permute-start | bytes 983048 | tf_op jit(solution)/shard_map/ppermute | solution.py:20
  361.3 11.4 %collective-permute-done.5 = f32[128,640]{1,0:T(8,128)S(1)} collective-permute-done((f32[128,640]{1,0:T(8,128)S(1)}, f32[128,640]{1,0:T(8,128)S(1)}, u32[]{:S(2)}, u32[]{:S(2)}) %collective-permute-start.5) | collective-permute-done | bytes 327712 | tf_op jit(solution)/shard_map/ppermute | solution.py:20
  372.7 1.5 fusion.61
  374.2 46.5 %all-gather.19.cloned.1.call-done = f32[4096,256]{1,0:T(8,128)} async-done(((f32[256,256]{1,0:T(8,128)}), f32[4096,256]{1,0:T(8,128)}) %all-gather.19.cloned.1.call-update) | async-done | bytes 4194320 | tf_op jit(solution)/shard_map/all_gather | solution.py:103
  420.7 2.5 reduce_sum.156
  424.5 0.7 multiply_reduce_fusion
  (142 shorter events, 49.4 us)
Async XLA Ops:
  6.5 30.1 %copy-start = (bf16[1024,128]{1,0:T(8,128)(2,1)S(1)}, bf16[1024,128]{1,0:T(8,128)(2,1)}, u32[]{:S(2)}) copy-start(bf16[1024,128]{1,0:T(8,128)(2,1)} %param.10) | copy-start | bytes 786436
  6.5 117.9 %all-gather.11.cloned.1.call-start = ((), (), s32[]{:S(2)}) async-start(), calls=%async_computation | async-start | bytes 4456448 | tf_op jit(solution)/shard_map/all_gather | solution.py:103
  7.5 7.7 %collective-permute-start = (bf16[79,640]{1,0:T(8,128)(2,1)S(1)}, bf16[79,640]{1,0:T(8,128)(2,1)S(1)}, u32[]{:S(2)}, u32[]{:S(2)}) collective-permute-start(bf16[79,640]{1,0:T(8,128)(2,1)S(1)} %slice.51), channel_id=1, source_target_pairs={{0,16},{16,32},{32,48},{48,64},{64,80},{80,96},{96,112},{112,128},... | collective-permute-start | bytes 303368 | tf_op jit(solution)/shard_map/ppermute | solution.py:14
  61.4 7.8 %collective-permute-start.1 = (f32[128,640]{1,0:T(8,128)S(1)}, f32[128,640]{1,0:T(8,128)S(1)}, u32[]{:S(2)}, u32[]{:S(2)}) collective-permute-start(f32[128,640]{1,0:T(8,128)S(1)} %fusion.52), channel_id=1, source_target_pairs={{0,16},{16,0},{32,48},{48,32},{64,80},{80,64},{96,112},{112,96},{1... | collective-permute-start | bytes 983048 | tf_op jit(solution)/shard_map/ppermute | solution.py:20
  70.8 124.3 %all-gather.13.cloned.1.call-start = ((), (), s32[]{:S(2)}) async-start(), calls=%async_computation.1 | async-start | bytes 4456448 | tf_op jit(solution)/shard_map/all_gather | solution.py:103
  133.1 2.7 copy-start.1
  137.0 12.4 %collective-permute-start.2 = (f32[128,640]{1,0:T(8,128)S(1)}, f32[128,640]{1,0:T(8,128)S(1)}, u32[]{:S(2)}, u32[]{:S(2)}) collective-permute-start(f32[128,640]{1,0:T(8,128)S(1)} %fusion.68), channel_id=1, source_target_pairs={{0,32},{16,48},{32,0},{48,16},{64,96},{80,112},{96,64},{112,80},{1... | collective-permute-start | bytes 983048 | tf_op jit(solution)/shard_map/ppermute | solution.py:20
  150.9 113.4 %all-gather.15.cloned.1.call-start = ((), (), s32[]{:S(2)}) async-start(), calls=%async_computation.2 | async-start | bytes 4456448 | tf_op jit(solution)/shard_map/all_gather | solution.py:103
  207.7 10.9 %collective-permute-start.3 = (f32[128,640]{1,0:T(8,128)S(1)}, f32[128,640]{1,0:T(8,128)S(1)}, u32[]{:S(2)}, u32[]{:S(2)}) collective-permute-start(f32[128,640]{1,0:T(8,128)S(1)} %fusion.66), channel_id=1, source_target_pairs={{0,64},{16,80},{32,96},{48,112},{64,0},{80,16},{96,32},{112,48},{1... | collective-permute-start | bytes 983048 | tf_op jit(solution)/shard_map/ppermute | solution.py:20
  220.1 121.3 %all-gather.17.cloned.1.call-start = ((), (), s32[]{:S(2)}) async-start(), calls=%async_computation.3 | async-start | bytes 4456448 | tf_op jit(solution)/shard_map/all_gather | solution.py:103
  276.9 18.8 %collective-permute-start.4 = (f32[128,640]{1,0:T(8,128)S(1)}, f32[128,640]{1,0:T(8,128)S(1)}, u32[]{:S(2)}, u32[]{:S(2)}) collective-permute-start(f32[128,640]{1,0:T(8,128)S(1)} %fusion.64), channel_id=1, source_target_pairs={{0,128},{16,144},{32,160},{48,176},{64,192},{80,208},{96,224},{112... | collective-permute-start | bytes 983048 | tf_op jit(solution)/shard_map/ppermute | solution.py:20
  297.2 123.5 %all-gather.19.cloned.1.call-start = ((), (), s32[]{:S(2)}) async-start(), calls=%async_computation.4 | async-start | bytes 4456448 | tf_op jit(solution)/shard_map/all_gather | solution.py:103
  354.0 18.7 %collective-permute-start.5 = (f32[128,640]{1,0:T(8,128)S(1)}, f32[128,640]{1,0:T(8,128)S(1)}, u32[]{:S(2)}, u32[]{:S(2)}) collective-permute-start(f32[128,640]{1,0:T(8,128)S(1)} %fusion.62), channel_id=1, source_target_pairs={{0,256},{16,272},{32,288},{48,304},{64,320},{80,336},{96,352},{112... | collective-permute-start | bytes 983048 | tf_op jit(solution)/shard_map/ppermute | solution.py:20
Sparse Core Ops, SparseCore 0:
  70.9 53.4 all-gather.10
  151.0 44.0 all-gather.12
  220.2 44.0 all-gather.14
  297.4 44.0 all-gather.16
  374.4 46.3 all-gather.18
